TPU v7x, 32 devices: a whole 2x2x4 slice. The times are simulated.
32 devices in a mesh: gy: 16 (over z, y, core), gz: 2 (over x).
Axes of the slice: x: 2, y: 2, z: 4, core: 2. Of those that a mesh axis runs over, the one named last changes fastest.
Arguments:
- initial_block: bfloat16 [16, 2, 2, 512, 512], P('gy', 'gz'), may hold values from -6 to 6
- tile_ops: bfloat16 [16, 2, 2, 512, 512], P('gy', 'gz'), may hold values from -0.125 to 0.125
- couple_ops: bfloat16 [16, 2, 4, 2, 512, 512], P('gy', 'gz'), may hold values from -0.125 to 0.125
- couple_map: int32 [16, 2, 4, 2], P('gy', 'gz'), may hold values from 0 to 1
- cell_scale: float32 [16, 2, 2, 512], P('gy', 'gz'), may hold values from 0.4 to 2.5
Outputs:
- basis: float32 [16, 2, 2, 512, 512], P('gy', 'gz')
- factor: float32 [512, 512], replicated
All inputs are finite; a program needn't handle non-finite values.
Results may differ from a plain program's by a relative error of at most 0.0053.
Values may be sent and summed in bfloat16 or wider, within the bound.
A program may use at most 64 MiB of HBM per device.

v0:
```python
import jax
import jax.numpy as jnp
from jax import lax
from jax.sharding import PartitionSpec as P


def shifted(block, axis, distance):
    devices = range(lax.axis_size(axis))
    route = [((i - distance) % len(devices), i) for i in devices]
    return lax.ppermute(block, axis, route)


def pick_tiles(blocks, indices):
    return jnp.take(blocks, indices, axis=0)


def neighbour_faces(scaled):
    y_from_lower = shifted(scaled, "gy", 1)
    y_from_upper = shifted(scaled, "gy", -1)
    z_from_lower = shifted(scaled, "gz", 1)
    z_from_upper = shifted(scaled, "gz", -1)
    faces = [y_from_lower[0, 0], y_from_upper[0, 0], z_from_lower[0, 0], z_from_upper[0, 0]]
    return jnp.stack(faces)


def apply_scaled(field, tile_ops, couple_ops, couple_map, cell_scale):
    scale_wide = cell_scale[..., None]
    scaled = (scale_wide * field).astype(jnp.bfloat16)
    inner = jnp.einsum(
        "tij,tjk->tik", tile_ops[0, 0], scaled[0, 0], preferred_element_type=jnp.float32
    )
    stacked = neighbour_faces(scaled)
    picked = jax.vmap(pick_tiles)(stacked, couple_map[0, 0])
    outer = jnp.einsum(
        "dtij,dtjk->tik", couple_ops[0, 0], picked, preferred_element_type=jnp.float32
    )
    return scale_wide * (inner + outer)[None, None]


def body(initial_block, tile_ops, couple_ops, couple_map, cell_scale):

    def filter_map(field):
        return (
            (1.0 - 1.1) * field - apply_scaled(field, tile_ops, couple_ops, couple_map, cell_scale)
        ) / 0.9

    first = initial_block.astype(jnp.float32)
    second = filter_map(first)
    third = 2.0 * filter_map(second) - first
    fourth = 2.0 * filter_map(third) - second
    width = fourth.shape[-1]
    flat = fourth.reshape(-1, width)
    total_cells = flat.shape[0] * lax.axis_size("gy") * lax.axis_size("gz")
    local_gram = jnp.einsum("ck,cl->kl", flat, flat, precision=lax.Precision.HIGHEST)
    gram = lax.psum(local_gram, ("gy", "gz"))
    gram = gram / jnp.float32(total_cells)
    lower = jnp.linalg.cholesky(gram)
    basis = jax.scipy.linalg.solve_triangular(lower, flat.T, lower=True).T
    return (basis.reshape(fourth.shape), lower.T)


def solution(mesh):
    placed = (
        P("gy", "gz", None, None, None),
        P("gy", "gz", None, None, None),
        P("gy", "gz", None, None, None, None),
        P("gy", "gz", None, None),
        P("gy", "gz", None, None),
    )
    return jax.shard_map(
        body,
        mesh=mesh,
        in_specs=placed,
        out_specs=(P("gy", "gz", None, None, None), P()),
        check_vma=False,
    )
```

profile of v0, /device:TPU:0, one launch (start us, length us, event | category | flops | bytes accessed | tf_op | source)
XLA Modules:
  0.0 432.9 jit_solution(8653095912852456125)
XLA Ops:
  7.2 1.6 fusion.10
  8.8 0.5 collective-permute-start
  9.4 5.0 %collective-permute-start.1 = (bf16[1,1,2,512,512]{4,3,2,1,0:T(8,128)(2,1)S(1)}, bf16[1,1,2,512,512]{4,3,2,1,0:T(8,128)(2,1)}, u32[]{:S(2)}, u32[]{:S(2)}) collective-permute-start(bf16[1,1,2,512,512]{4,3,2,1,0:T(8,128)(2,1)S(1)} %fusion.10), channel_id=1, source_target_pairs={{2,0},{4,2},{6,4},{8,6},{10,8},{12,10},{14,12},{16,14},{18,16},{20... | collective-permute-start | bytes 3145736 | tf_op jit(solution)/shard_map/ppermute | solution.py:10
  14.4 1.9 collective-permute-start.2
  16.5 2.0 fusion.48
  18.6 8.4 %collective-permute-done = bf16[1,1,2,512,512]{4,3,2,1,0:T(8,128)(2,1)S(1)} collective-permute-done((bf16[1,1,2,512,512]{4,3,2,1,0:T(8,128)(2,1)S(1)}, bf16[1,1,2,512,512]{4,3,2,1,0:T(8,128)(2,1)S(1)}, u32[]{:S(2)}, u32[]{:S(2)}) %collective-permute-start) | collective-permute-done | bytes 1048608 | tf_op jit(solution)/shard_map/ppermute | solution.py:10
  27.0 10.2 %collective-permute-done.2 = bf16[1,1,2,512,512]{4,3,2,1,0:T(8,128)(2,1)} collective-permute-done((bf16[1,1,2,512,512]{4,3,2,1,0:T(8,128)(2,1)S(1)}, bf16[1,1,2,512,512]{4,3,2,1,0:T(8,128)(2,1)}, u32[]{:S(2)}, u32[]{:S(2)}) %collective-permute-start.2) | collective-permute-done | bytes 1048608 | tf_op jit(solution)/shard_map/ppermute | solution.py:10
  37.2 3.9 pad_maximum_fusion
  41.1 5.1 %gather_fusion = bf16[8,512,512]{2,1,0:T(8,128)(2,1)} fusion(bf16[4,2,512,512]{3,2,1,0:T(8,128)(2,1)} %pad_maximum_fusion, s32[8]{0:T(128)S(1)} %reshape.120), kind=kCustom, calls=%fused_computation.clone | custom fusion | bytes 8388672 | tf_op jit(solution)/shard_map/vmap(jit(_take))/gather | solution.py:14
  46.2 7.5 %multiply_convert_fusion.1 = (bf16[1,1,2,512,512]{4,3,2,1,0:T(8,128)(2,1)S(1)}, f32[1,1,2,512,512]{4,3,2,1,0:T(8,128)}) fusion(f32[2,512]{1,0:T(2,128)S(1)} %broadcast_multiply_fusion.1, f32[2,512,512]{1,2,0:T(8,128)S(1)} %copy-done.4, bf16[4,2,512,512]{3,2,1,0:T(8,128)(2,1)} %bitcast.157, pred[4,2]{0,1:T(4,128)(4,1)S(1)} %compare_and_fusion, ...), kind=kOutput, calls=%fused_computation.43 | convolution fusion | flops 2153250816 | bytes 14688264 | tf_op jit(solution)/shard_map/dtij,dtjk->tik/dot_general | solution.py:34
  53.8 0.4 collective-permute-start.3
  54.2 4.0 collective-permute-start.4
  58.2 1.5 collective-permute-start.5
  59.7 0.7 fusion.46
  60.4 10.4 %collective-permute-done.3 = bf16[1,1,2,512,512]{4,3,2,1,0:T(8,128)(2,1)S(1)} collective-permute-done((bf16[1,1,2,512,512]{4,3,2,1,0:T(8,128)(2,1)S(1)}, bf16[1,1,2,512,512]{4,3,2,1,0:T(8,128)(2,1)S(1)}, u32[]{:S(2)}, u32[]{:S(2)}) %collective-permute-start.3) | collective-permute-done | bytes 1048608 | tf_op jit(solution)/shard_map/ppermute | solution.py:10
  70.8 9.7 %collective-permute-done.5 = bf16[1,1,2,512,512]{4,3,2,1,0:T(8,128)(2,1)S(1)} collective-permute-done((bf16[1,1,2,512,512]{4,3,2,1,0:T(8,128)(2,1)S(1)}, bf16[1,1,2,512,512]{4,3,2,1,0:T(8,128)(2,1)S(1)}, u32[]{:S(2)}, u32[]{:S(2)}) %collective-permute-start.5) | collective-permute-done | bytes 1048608 | tf_op jit(solution)/shard_map/ppermute | solution.py:10
  80.5 2.3 pad_maximum_fusion.1
  82.7 4.9 %gather_fusion.1 = bf16[8,512,512]{2,1,0:T(8,128)(2,1)} fusion(bf16[4,2,512,512]{3,2,1,0:T(8,128)(2,1)} %pad_maximum_fusion.1, s32[8]{0:T(128)S(1)} %reshape.120), kind=kCustom, calls=%fused_computation.1.clone | custom fusion | bytes 8388672 | tf_op jit(solution)/shard_map/vmap(jit(_take))/gather | solution.py:14
  87.7 8.4 %multiply_convert_fusion = (bf16[1,1,2,512,512]{4,3,2,1,0:T(8,128)(2,1)S(1)}, f32[1,1,2,512,512]{4,3,2,1,0:T(8,128)}) fusion(f32[2,512]{1,0:T(2,128)S(1)} %bitcast.173, bf16[1,1,2,512,512]{4,3,2,1,0:T(8,128)(2,1)} %param.7, f32[2,512,512]{1,2,0:T(8,128)S(1)} %fusion.46, bf16[4,2,512,512]{3,2,1,0:T(8,128)(2,1)} %bitcast.158, ...), kind=kOutput, calls=%fused_computation.42 | convolution fusion | flops 2154299392 | bytes 16781320 | tf_op jit(solution)/shard_map/dtij,dtjk->tik/dot_general | solution.py:34
  96.1 0.4 collective-permute-start.6
  96.5 4.0 collective-permute-start.7
  100.6 1.5 collective-permute-start.8
  102.0 0.7 fusion.44
  102.8 10.4 %collective-permute-done.6 = bf16[1,1,2,512,512]{4,3,2,1,0:T(8,128)(2,1)S(1)} collective-permute-done((bf16[1,1,2,512,512]{4,3,2,1,0:T(8,128)(2,1)S(1)}, bf16[1,1,2,512,512]{4,3,2,1,0:T(8,128)(2,1)S(1)}, u32[]{:S(2)}, u32[]{:S(2)}) %collective-permute-start.6) | collective-permute-done | bytes 1048608 | tf_op jit(solution)/shard_map/ppermute | solution.py:10
  113.1 9.7 %collective-permute-done.8 = bf16[1,1,2,512,512]{4,3,2,1,0:T(8,128)(2,1)S(1)} collective-permute-done((bf16[1,1,2,512,512]{4,3,2,1,0:T(8,128)(2,1)S(1)}, bf16[1,1,2,512,512]{4,3,2,1,0:T(8,128)(2,1)S(1)}, u32[]{:S(2)}, u32[]{:S(2)}) %collective-permute-start.8) | collective-permute-done | bytes 1048608 | tf_op jit(solution)/shard_map/ppermute | solution.py:10
  122.8 2.7 pad_maximum_fusion.2
  125.5 4.9 %gather_fusion.2 = bf16[8,512,512]{2,1,0:T(8,128)(2,1)} fusion(bf16[4,2,512,512]{3,2,1,0:T(8,128)(2,1)} %pad_maximum_fusion.2, s32[8]{0:T(128)S(1)} %reshape.120), kind=kCustom, calls=%fused_computation.2.clone | custom fusion | bytes 8388672 | tf_op jit(solution)/shard_map/vmap(jit(_take))/gather | solution.py:14
  130.5 7.3 %fusion.12 = f32[1,1,2,512,512]{4,3,2,1,0:T(8,128)S(1)} fusion(f32[2,512,512]{1,2,0:T(8,128)S(1)} %fusion.44, f32[1,1,2,512,512]{4,3,2,1,0:T(8,128)} %get-tuple-element.38, f32[1,1,2,512,512]{4,3,2,1,0:T(8,128)} %get-tuple-element.40, bf16[4,2,512,512]{3,2,1,0:T(8,128)(2,1)} %bitcast.156, pred[4,2]{0,1:T(4,128)(4,1)S(1)} %compare_and_fusion, ...), kind=kOutput, calls=%fused_computation.28 | convolution fusion | flops 2153250816 | bytes 16781320 | tf_op jit(solution)/shard_map/dtij,dtjk->tik/dot_general | solution.py:34
  137.8 1.3 copy-done.3
  139.1 4.5 %fusion.28 = f32[512,512]{0,1:T(8,128)} fusion(f32[1,1,2,512,512]{4,3,2,1,0:T(8,128)S(1)} %fusion.12), kind=kOutput, calls=%fused_computation.50 | convolution fusion | flops 3221225472 | bytes 3145728 | tf_op jit(solution)/shard_map/ck,cl->kl/dot_general | solution.py:54
  143.7 130.7 %all-reduce.3.cloned.1.call-done = f32[512,512]{0,1:T(8,128)} async-done(((f32[512,512]{0,1:T(8,128)}), f32[512,512]{0,1:T(8,128)}) %all-reduce.3.cloned.1.call-update) | async-done | bytes 1048592 | tf_op jit(solution)/shard_map/psum | solution.py:55
  274.4 1.4 broadcast_multiply_fusion
  276.4 11.7 %cholesky.104 = f32[128,128]{1,0:T(8,128)S(1)} custom-call(f32[128,128]{1,0:T(8,128)S(1)} %cholesky.266), custom_call_target="Cholesky" | custom-call | tf_op jit(solution)/shard_map/jit(cholesky)/cholesky | solution.py:57
  288.3 10.0 %custom-call.31 = f32[1,128,128]{1,2,0:T(8,128)S(1)} custom-call(f32[1,128,128]{2,1,0:T(8,128)S(1)} %get-tuple-element.36), custom_call_target="InvertDiagBlocksLowerTriangular" | custom-call | tf_op jit(solution)/shard_map/jit(cholesky)/cholesky | solution.py:57
  298.9 11.7 %cholesky.217 = f32[128,128]{1,0:T(8,128)S(1)} custom-call(f32[128,128]{1,0:T(8,128)S(1)} %cholesky.270), custom_call_target="Cholesky" | custom-call | tf_op jit(solution)/shard_map/jit(cholesky)/cholesky | solution.py:57
  310.7 9.8 %custom-call.32 = f32[1,128,128]{1,2,0:T(8,128)S(1)} custom-call(f32[1,128,128]{2,1,0:T(8,128)S(1)} %get-tuple-element.33), custom_call_target="InvertDiagBlocksLowerTriangular" | custom-call | tf_op jit(solution)/shard_map/jit(cholesky)/cholesky | solution.py:57
  320.8 0.4 convolution_subtract_fusion.3
  321.2 11.7 %cholesky.238 = f32[128,128]{1,0:T(8,128)S(1)} custom-call(f32[128,128]{1,0:T(8,128)S(1)} %cholesky.275), custom_call_target="Cholesky" | custom-call | tf_op jit(solution)/shard_map/jit(cholesky)/cholesky | solution.py:57
  332.9 0.7 compare_reduce_fusion.1
  333.6 10.0 %custom-call.33 = f32[1,128,128]{1,2,0:T(8,128)S(1)} custom-call(f32[1,128,128]{2,1,0:T(8,128)S(1)} %get-tuple-element.30), custom_call_target="InvertDiagBlocksLowerTriangular" | custom-call | tf_op jit(solution)/shard_map/jit(cholesky)/cholesky | solution.py:57
  343.8 0.4 convolution_subtract_fusion.4
  344.2 11.7 %cholesky.255 = f32[128,128]{1,0:T(8,128)S(1)} custom-call(f32[128,128]{1,0:T(8,128)S(1)} %convolution_subtract_fusion.4), custom_call_target="Cholesky" | custom-call | tf_op jit(solution)/shard_map/jit(cholesky)/cholesky | solution.py:57
  355.9 0.7 compare_reduce_fusion
  356.6 0.6 compare_reduce_fusion.2
  359.6 1.2 fusion.54
  360.9 8.4 %while.1 = (s32[]{:T(128)}, f32[512,512]{1,0:T(8,128)S(1)}, s32[4,2]{0,1:T(2,128)S(1)}, f32[4,128,128]{2,1,0:T(8,128)S(1)}, s32[]{:T(128)}) while((s32[]{:T(128)}, f32[512,512]{1,0:T(8,128)S(1)}, s32[4,2]{0,1:T(2,128)S(1)}, f32[4,128,128]{2,1,0:T(8,128)S(1)}, s32[]{:T(128)}) %tuple.37), condition=%wide.while_cond, body=%wide.while_body.sunk | while | flops 2 | bytes 131181 | solution.py:58
  361.0 0.6 fusion.89
  361.5 1.4 bitcast_dynamic-update-slice_fusion.2
  363.1 0.6 fusion.89
  363.6 1.4 bitcast_dynamic-update-slice_fusion.2
  365.2 0.6 fusion.89
  365.7 1.4 bitcast_dynamic-update-slice_fusion.2
  367.3 0.6 fusion.89
  367.8 1.4 bitcast_dynamic-update-slice_fusion.2
  369.3 39.6 %custom-call.34 = f32[4,128,128]{1,2,0:T(8,128)S(1)} custom-call(f32[4,128,128]{2,1,0:T(8,128)S(1)} %get-tuple-element.10), custom_call_target="InvertDiagBlocksLowerTriangular" | custom-call | tf_op jit(solution)/shard_map/jit(_solve_triangular)/triangular_solve | solution.py:58
  408.9 1.7 fusion.55
  410.6 2.0 convolution_subtract_fusion.1
  412.6 0.6 fusion.68
  413.2 2.9 convolution_subtract_fusion
  416.1 0.6 fusion.66
  416.7 3.8 fusion.37
  420.5 0.6 fusion.65
  421.3 1.8 copy.41
  423.1 2.5 copy.34
  (45 shorter events, 2.7 us)
Async XLA Ops:
  7.2 9.4 %copy-start = (bf16[1,1,2,512,512]{4,3,2,1,0:T(8,128)(2,1)S(1)}, bf16[1,1,2,512,512]{4,3,2,1,0:T(8,128)(2,1)}, u32[]{:S(2)}) copy-start(bf16[1,1,2,512,512]{4,3,2,1,0:T(8,128)(2,1)} %param.8) | copy-start | bytes 3145732
  7.2 9.3 %copy-start.5 = (f32[1,1,2,512]{3,2,1,0:T(2,128)S(1)}, f32[1,1,2,512]{3,2,1,0:T(2,128)}, u32[]{:S(2)}) copy-start(f32[1,1,2,512]{3,2,1,0:T(2,128)} %param.11) | copy-start | bytes 12292
  7.2 9.1 %copy-start.6 = (s32[1,1,4,2]{2,3,1,0:T(2,128)S(1)}, s32[1,1,4,2]{2,3,1,0:T(2,128)}, u32[]{:S(2)}) copy-start(s32[1,1,4,2]{2,3,1,0:T(2,128)} %param.10) | copy-start | bytes 100
  7.2 267.2 %all-reduce.3.cloned.1.call-start = ((), (), s32[]{:S(2)}) async-start(), calls=%async_computation | async-start | bytes 2097152 | tf_op jit(solution)/shard_map/psum | solution.py:55
  8.8 18.1 %collective-permute-start = (bf16[1,1,2,512,512]{4,3,2,1,0:T(8,128)(2,1)S(1)}, bf16[1,1,2,512,512]{4,3,2,1,0:T(8,128)(2,1)S(1)}, u32[]{:S(2)}, u32[]{:S(2)}) collective-permute-start(bf16[1,1,2,512,512]{4,3,2,1,0:T(8,128)(2,1)S(1)} %fusion.10), channel_id=1, source_target_pairs={{30,0},{0,2},{2,4},{4,6},{6,8},{8,10},{10,12},{12,14},{14,16},{16,... | collective-permute-start | bytes 3145736 | tf_op jit(solution)/shard_map/ppermute | solution.py:10
  9.4 17.6 %collective-permute-start.1 = (bf16[1,1,2,512,512]{4,3,2,1,0:T(8,128)(2,1)S(1)}, bf16[1,1,2,512,512]{4,3,2,1,0:T(8,128)(2,1)}, u32[]{:S(2)}, u32[]{:S(2)}) collective-permute-start(bf16[1,1,2,512,512]{4,3,2,1,0:T(8,128)(2,1)S(1)} %fusion.10), channel_id=1, source_target_pairs={{2,0},{4,2},{6,4},{8,6},{10,8},{12,10},{14,12},{16,14},{18,16},{20... | collective-permute-start | bytes 3145736 | tf_op jit(solution)/shard_map/ppermute | solution.py:10
  14.4 22.7 %collective-permute-start.2 = (bf16[1,1,2,512,512]{4,3,2,1,0:T(8,128)(2,1)S(1)}, bf16[1,1,2,512,512]{4,3,2,1,0:T(8,128)(2,1)}, u32[]{:S(2)}, u32[]{:S(2)}) collective-permute-start(bf16[1,1,2,512,512]{4,3,2,1,0:T(8,128)(2,1)S(1)} %fusion.10), channel_id=1, source_target_pairs={{1,0},{0,1},{3,2},{2,3},{5,4},{4,5},{7,6},{6,7},{9,8},{8,9},{11,10... | collective-permute-start | bytes 3145736 | tf_op jit(solution)/shard_map/ppermute | solution.py:10
  41.1 5.1 %copy-start.4 = (f32[2,512,512]{1,2,0:T(8,128)S(1)}, f32[2,512,512]{1,2,0:T(8,128)}, u32[]{:S(2)}) copy-start(f32[2,512,512]{1,2,0:T(8,128)} %fusion.48) | copy-start | bytes 6291460
  53.8 17.0 %collective-permute-start.3 = (bf16[1,1,2,512,512]{4,3,2,1,0:T(8,128)(2,1)S(1)}, bf16[1,1,2,512,512]{4,3,2,1,0:T(8,128)(2,1)S(1)}, u32[]{:S(2)}, u32[]{:S(2)}) collective-permute-start(bf16[1,1,2,512,512]{4,3,2,1,0:T(8,128)(2,1)S(1)} %get-tuple-element.37), channel_id=1, source_target_pairs={{30,0},{0,2},{2,4},{4,6},{6,8},{8,10},{10,12},{12,14},{14,16},{16,... | collective-permute-start | bytes 3145736 | tf_op jit(solution)/shard_map/ppermute | solution.py:10
  54.2 16.6 %collective-permute-start.4 = (bf16[1,1,2,512,512]{4,3,2,1,0:T(8,128)(2,1)S(1)}, bf16[1,1,2,512,512]{4,3,2,1,0:T(8,128)(2,1)S(1)}, u32[]{:S(2)}, u32[]{:S(2)}) collective-permute-start(bf16[1,1,2,512,512]{4,3,2,1,0:T(8,128)(2,1)S(1)} %get-tuple-element.37), channel_id=1, source_target_pairs={{2,0},{4,2},{6,4},{8,6},{10,8},{12,10},{14,12},{16,14},{18,16},{20... | collective-permute-start | bytes 3145736 | tf_op jit(solution)/shard_map/ppermute | solution.py:10
  58.2 22.3 %collective-permute-start.5 = (bf16[1,1,2,512,512]{4,3,2,1,0:T(8,128)(2,1)S(1)}, bf16[1,1,2,512,512]{4,3,2,1,0:T(8,128)(2,1)S(1)}, u32[]{:S(2)}, u32[]{:S(2)}) collective-permute-start(bf16[1,1,2,512,512]{4,3,2,1,0:T(8,128)(2,1)S(1)} %get-tuple-element.37), channel_id=1, source_target_pairs={{1,0},{0,1},{3,2},{2,3},{5,4},{4,5},{7,6},{6,7},{9,8},{8,9},{11,10... | collective-permute-start | bytes 3145736 | tf_op jit(solution)/shard_map/ppermute | solution.py:10
  96.1 17.0 %collective-permute-start.6 = (bf16[1,1,2,512,512]{4,3,2,1,0:T(8,128)(2,1)S(1)}, bf16[1,1,2,512,512]{4,3,2,1,0:T(8,128)(2,1)S(1)}, u32[]{:S(2)}, u32[]{:S(2)}) collective-permute-start(bf16[1,1,2,512,512]{4,3,2,1,0:T(8,128)(2,1)S(1)} %get-tuple-element.39), channel_id=1, source_target_pairs={{30,0},{0,2},{2,4},{4,6},{6,8},{8,10},{10,12},{12,14},{14,16},{16,... | collective-permute-start | bytes 3145736 | tf_op jit(solution)/shard_map/ppermute | solution.py:10
  96.5 16.6 %collective-permute-start.7 = (bf16[1,1,2,512,512]{4,3,2,1,0:T(8,128)(2,1)S(1)}, bf16[1,1,2,512,512]{4,3,2,1,0:T(8,128)(2,1)S(1)}, u32[]{:S(2)}, u32[]{:S(2)}) collective-permute-start(bf16[1,1,2,512,512]{4,3,2,1,0:T(8,128)(2,1)S(1)} %get-tuple-element.39), channel_id=1, source_target_pairs={{2,0},{4,2},{6,4},{8,6},{10,8},{12,10},{14,12},{16,14},{18,16},{20... | collective-permute-start | bytes 3145736 | tf_op jit(solution)/shard_map/ppermute | solution.py:10
  100.6 22.3 %collective-permute-start.8 = (bf16[1,1,2,512,512]{4,3,2,1,0:T(8,128)(2,1)S(1)}, bf16[1,1,2,512,512]{4,3,2,1,0:T(8,128)(2,1)S(1)}, u32[]{:S(2)}, u32[]{:S(2)}) collective-permute-start(bf16[1,1,2,512,512]{4,3,2,1,0:T(8,128)(2,1)S(1)} %get-tuple-element.39), channel_id=1, source_target_pairs={{1,0},{0,1},{3,2},{2,3},{5,4},{4,5},{7,6},{6,7},{9,8},{8,9},{11,10... | collective-permute-start | bytes 3145736 | tf_op jit(solution)/shard_map/ppermute | solution.py:10
  137.8 1.3 copy-start.3
  274.4 1.8 copy-start.2
  421.3 4.4 %copy-start.1 = (bf16[1,1,2,512,512]{4,3,2,1,0:T(8,128)(2,1)S(1)}, bf16[1,1,2,512,512]{4,3,2,1,0:T(8,128)(2,1)}, u32[]{:S(2)}) copy-start(bf16[1,1,2,512,512]{4,3,2,1,0:T(8,128)(2,1)} %param.8) | copy-start | bytes 3145732
Sparse Core Ops, SparseCore 0:
  143.8 130.5 all-reduce.2
where the time goes:
time: 439 us; the launch traced here: 433 us
  waiting for transfers between devices  189 us (43%)
  other arithmetic  132 us (30%)
  matrix products  45.4 us (10%)
  local copies, waits for them, and re-layouts  29.7 us (7%)
  starting transfers between devices  19.4 us (4%)
  between operations  17.2 us (4%)
    psum x1, waiting for transfers between devices, body(): gram = lax.psum(local_gram, ('gy', 'gz'))  131 us
    another operation x14, other arithmetic, body(): lower = jnp.linalg.cholesky(gram)  78.7 us
    ppermute x9, waiting for transfers between devices, shifted(): return lax.ppermute(block, axis, route)  58.7 us
    another operation x2, other arithmetic, body(): basis = jax.scipy.linalg.solve_triangular(lower, flat.T, lower=True).T  39.6 us
    dot_general x3, matrix products, apply_scaled(): jnp.einsum('dtij,dtjk->tik', couple_ops[0, 0], picked, preferred_element_...  23.3 us
    ppermute x9, starting transfers between devices, shifted(): return lax.ppermute(block, axis, route)  19.3 us
    gather x5, local copies, waits for them, and re-layouts, pick_tiles(): return jnp.take(blocks, indices, axis=0)  15.2 us
    another operation x7, matrix products, body(): basis = jax.scipy.linalg.solve_triangular(lower, flat.T, lower=True).T  12.2 us
  transfers between devices with their start and end apart: 10, of which 7 were waited for; matrix products, arithmetic and copies ran while one was open for 1% of the time, Pallas kernels for 0%

commit v1 on v0

v1 whole, which is shorter than its diff:
```python
import functools

import jax
import jax.numpy as jnp
from jax import lax
from jax.experimental import pallas as pl
from jax.experimental.pallas import tpu as pltpu
from jax.sharding import PartitionSpec as P

F32, BF16 = jnp.float32, jnp.bfloat16
MESH = pl.DeviceIdType.MESH
ROUNDS = 3
CHUNKS = 2
BASE = 128
PANEL = 8


def split(x):
    hi = x.astype(BF16)
    return hi, (x - hi.astype(F32)).astype(BF16)


def xor_stages(ny, nz, rows):
    order = [("gy", 0)]
    order += [("gz", b) for b in range(nz.bit_length() - 1)]
    order += [("gy", b) for b in range(1, ny.bit_length() - 1)]
    stages, size = [], rows
    for axis, bit in order:
        halve = size % 16 == 0
        stages.append((axis, bit, size, halve))
        size = size // 2 if halve else size
    return stages


def filter_kernel(
    ny, nz, stages, nvec,
    map_ref, scale_ref, first_ref, tile_hbm, couple_hbm,
    y_ref, gram_ref,
    tile_ref, couple_ref, sent, second, third, hi, lo, gsum, gall, *rest,
):
    pieces, rest = rest[: len(stages)], rest[len(stages):]
    op_sem, send_sem, recv_sem, rs_send, rs_recv, ag_send, ag_recv, *landed = rest
    got = {
        (d, r, c): landed[(d * ROUNDS + r) * CHUNKS + c]
        for d in range(len(landed) // (ROUNDS * CHUNKS)) for r in range(ROUNDS) for c in range(CHUNKS)
    }
    tiles, cells, width = first_ref.shape
    cw = width // CHUNKS
    iy, iz = lax.axis_index("gy"), lax.axis_index("gz")
    where = {"gy": iy, "gz": iz}

    def partner(axis, bit):
        me = where[axis]
        b = (me // (2**bit)) % 2
        return {axis: me + (1 - 2 * b) * (2**bit)}, b

    targets = [{"gy": (iy + 1) % ny}, {"gy": (iy + ny - 1) % ny}]
    if nz == 2:
        targets.append({"gz": 1 - iz})
        slot = (0, 1, 2, 2)
    else:
        targets += [{"gz": (iz + 1) % nz}, {"gz": (iz + nz - 1) % nz}]
        slot = (0, 1, 2, 3)

    copies_in = [
        pltpu.make_async_copy(tile_hbm, tile_ref, op_sem.at[0]),
        pltpu.make_async_copy(couple_hbm, couple_ref, op_sem.at[1]),
    ]
    for copy in copies_in:
        copy.start()

    barrier = pltpu.get_barrier_semaphore()
    greeted = targets + [partner(axis, bit)[0] for axis, bit, _, _ in stages]
    for other in greeted:
        pl.semaphore_signal(barrier, inc=1, device_id=other, device_id_type=MESH)

    def send(r, c):
        made = []
        for d, other in enumerate(targets):
            copy = pltpu.make_async_remote_copy(
                src_ref=sent.at[r, c],
                dst_ref=got[d, r, c],
                send_sem=send_sem.at[d, r, c],
                recv_sem=recv_sem.at[d, r, c],
                device_id=other,
                device_id_type=MESH,
            )
            copy.start()
            made.append(copy)
        return made

    moving = {}
    for c in range(CHUNKS):
        for t in range(tiles):
            sent[0, c, t] = (scale_ref[t] * first_ref[t, :, c * cw:(c + 1) * cw].astype(F32)).astype(BF16)
        if c == 0:
            pl.semaphore_wait(barrier, len(greeted))
        moving[0, c] = send(0, c)
    for copy in copies_in:
        copy.wait()

    def gram_of(i, j, place):
        def dot(a, b):
            return lax.dot_general(a, b, (((0,), (0,)), ((), ())), preferred_element_type=F32)
        left, right = slice(i * cw, (i + 1) * cw), slice(j * cw, (j + 1) * cw)
        total = dot(hi[:, left], hi[:, right])
        total += dot(hi[:, left], lo[:, right])
        total += dot(lo[:, left], hi[:, right])
        gsum[place * cw:(place + 1) * cw] = total

    for r in range(ROUNDS):
        for c in range(CHUNKS):
            for copy in moving[r, c]:
                copy.wait_recv()
            cols = slice(c * cw, (c + 1) * cw)

            def one(t, carry, r=r, c=c, cols=cols):
                acc = jnp.dot(tile_ref[t], sent[r, c, t], preferred_element_type=F32)
                for d in range(4):
                    acc += jnp.dot(
                        couple_ref[d, t], got[slot[d], r, c][map_ref[d, t]], preferred_element_type=F32
                    )
                s = scale_ref[t]
                if r == 0:
                    y = first_ref[t, :, cols].astype(F32)
                elif r == 1:
                    y = second[c, t]
                else:
                    y = third[c, t]
                py = ((1.0 - 1.1) * y - s * acc) / 0.9
                if r == 0:
                    new = py
                    second[c, t] = new
                elif r == 1:
                    new = 2.0 * py - first_ref[t, :, cols].astype(F32)
                    third[c, t] = new
                else:
                    new = 2.0 * py - second[c, t]
                    y_ref[t, :, cols] = new
                    a, b = split(new)
                    here = pl.ds(pl.multiple_of(t * cells, cells), cells)
                    hi[here, cols] = a
                    lo[here, cols] = b
                if r < ROUNDS - 1:
                    sent[r + 1, c, t] = (s * new).astype(BF16)
                return carry

            lax.fori_loop(0, tiles, one, 0)
            if r < ROUNDS - 1:
                moving[r + 1, c] = send(r + 1, c)
            else:
                place = c * (c + 1) // 2
                for i in range(c + 1):
                    gram_of(i, c, place + i)

    base = 0
    for n, (axis, bit, size, halve) in enumerate(stages):
        other, b = partner(axis, bit)
        part = size // 2 if halve else size
        out = base + (1 - b) * part if halve else base
        keep = base + b * part if halve else base
        copy = pltpu.make_async_remote_copy(
            src_ref=gsum.at[pl.ds(pl.multiple_of(out, 8), part)],
            dst_ref=pieces[n],
            send_sem=rs_send.at[n],
            recv_sem=rs_recv.at[n],
            device_id=other,
            device_id_type=MESH,
        )
        copy.start()
        copy.wait()
        here = pl.ds(pl.multiple_of(keep, 8), part)
        gsum[here] = gsum[here] + pieces[n][...]
        base = keep
    last = stages[-1][2] // 2 if stages[-1][3] else stages[-1][2]
    here = pl.ds(pl.multiple_of(base, 8), last)
    gall[here] = gsum[here]
    for n in reversed(range(len(stages))):
        axis, bit, size, halve = stages[n]
        if not halve:
            continue
        other, b = partner(axis, bit)
        here = pl.ds(pl.multiple_of(base, 8), size // 2)
        copy = pltpu.make_async_remote_copy(
            src_ref=gall.at[here],
            dst_ref=gall.at[here],
            send_sem=ag_send.at[n],
            recv_sem=ag_recv.at[n],
            device_id=other,
            device_id_type=MESH,
        )
        copy.start()
        copy.wait()
        base = base - b * (size // 2)
    gram_ref[...] = gall[...]
    for made in moving.values():
        for copy in made:
            copy.wait_send()


def factor_block(work):
    sub = lax.broadcasted_iota(jnp.int32, (PANEL, BASE), 0)
    lane = lax.broadcasted_iota(jnp.int32, (PANEL, BASE), 1)

    def panel(p, carry):
        rows = pl.ds(pl.multiple_of(p * PANEL, PANEL), PANEL)
        left, right = work[rows, :BASE], work[rows, BASE:]
        turned = pltpu.roll(left, lax.rem(BASE - p * PANEL, BASE), 1)
        cols = [jnp.broadcast_to(turned[:, j:j + 1], (PANEL, BASE)) for j in range(PANEL)]
        scale = jnp.zeros((PANEL, BASE), F32)
        for i in range(PANEL):
            def row(x):
                return jnp.broadcast_to(x[i:i + 1], (PANEL, BASE))
            inv = lax.rsqrt(row(cols[i]))
            coef = jnp.where(sub > i, cols[i] * (inv * inv), 0.0)
            scale = jnp.where(sub == i, inv, scale)
            for j in range(i + 1, PANEL):
                cols[j] = cols[j] - coef * row(cols[j])
            left = left - coef * row(left)
            right = right - coef * row(right)
        left, right = left * scale, right * scale
        work[rows, :BASE] = left
        work[rows, BASE:] = right
        below = jnp.where(lane >= (p + 1) * PANEL, left, 0.0)
        both = jnp.concatenate([left, right], axis=1)
        work[...] = work[...] - lax.dot_general(
            below, both, (((0,), (0,)), ((), ())),
            precision=lax.Precision.HIGHEST, preferred_element_type=F32,
        )
        return carry

    lax.fori_loop(0, BASE // PANEL, panel, 0)


def ortho_kernel(total_cells, gram_ref, y_ref, basis_ref, factor_ref, full, work):
    width = factor_ref.shape[0]
    cw = width // CHUNKS
    count = width // BASE

    def dot(a, b, dims):
        return lax.dot_general(
            a, b, (dims, ((), ())), precision=lax.Precision.HIGHEST, preferred_element_type=F32
        )

    full[...] = jnp.zeros_like(full)
    for c in range(CHUNKS):
        for i in range(c + 1):
            place = c * (c + 1) // 2 + i
            full[i * cw:(i + 1) * cw, c * cw:(c + 1) * cw] = (
                gram_ref[place * cw:(place + 1) * cw] / jnp.float32(total_cells)
            )
    eye = (
        lax.broadcasted_iota(jnp.int32, (BASE, BASE), 0)
        == lax.broadcasted_iota(jnp.int32, (BASE, BASE), 1)
    ).astype(F32)
    for k in range(count):
        rows = slice(k * BASE, (k + 1) * BASE)
        full[rows, width + k * BASE:width + (k + 1) * BASE] = eye
        work[:, :BASE] = full[rows, rows]
        work[:, BASE:] = eye
        factor_block(work)
        full[rows, rows] = work[:, :BASE]
        mult = work[:, BASE:]
        beyond = slice((k + 1) * BASE, width + (k + 1) * BASE)
        new = dot(mult, full[rows, beyond], ((1,), (0,)))
        full[rows, beyond] = new
        for i in range(k + 1, count):
            here = slice(i * BASE, (i + 1) * BASE)
            span = slice(i * BASE, width + (k + 1) * BASE)
            full[here, span] = full[here, span] - dot(
                full[rows, here], full[rows, span], ((0,), (0,))
            )
    tri = lax.broadcasted_iota(jnp.int32, (width, width), 0) <= lax.broadcasted_iota(
        jnp.int32, (width, width), 1
    )
    factor_ref[...] = jnp.where(tri, full[:, :width], 0.0)
    ih, il = split(full[:, width:])

    def rows_of(n, carry):
        here = pl.ds(pl.multiple_of(n * 256, 256), 256)
        yh, yl = split(y_ref[here])

        def half(a, b):
            return lax.dot_general(a, b, (((1,), (1,)), ((), ())), preferred_element_type=F32)

        basis_ref[here] = half(yh, ih) + half(yh, il) + half(yl, ih)
        return carry

    lax.fori_loop(0, y_ref.shape[0] // 256, rows_of, 0)


def orthonormalize(gram, y, total_cells):
    width = y.shape[-1]
    return pl.pallas_call(
        functools.partial(ortho_kernel, total_cells),
        out_shape=(
            jax.ShapeDtypeStruct(y.shape, F32),
            jax.ShapeDtypeStruct((width, width), F32),
        ),
        in_specs=[pl.BlockSpec(memory_space=pltpu.VMEM)] * 2,
        out_specs=(pl.BlockSpec(memory_space=pltpu.VMEM),) * 2,
        scratch_shapes=[
            pltpu.VMEM((width, 2 * width), F32),
            pltpu.VMEM((BASE, 2 * BASE), F32),
        ],
        name="ortho",
    )(gram, y)


def body(ny, nz, initial_block, tile_ops, couple_ops, couple_map, cell_scale):
    shape = initial_block.shape
    tiles, cells, width = shape[2:]
    cw = width // CHUNKS
    packed = CHUNKS * (CHUNKS + 1) // 2 * cw
    stages = xor_stages(ny, nz, packed)
    ndir = 3 if nz == 2 else 4
    vm, any_ = pl.BlockSpec(memory_space=pltpu.VMEM), pl.BlockSpec(memory_space=pl.ANY)
    dma = pltpu.SemaphoreType.DMA
    y, gram = pl.pallas_call(
        functools.partial(filter_kernel, ny, nz, stages, width),
        out_shape=(
            jax.ShapeDtypeStruct((tiles, cells, width), F32),
            jax.ShapeDtypeStruct((packed, cw), F32),
        ),
        in_specs=[pl.BlockSpec(memory_space=pltpu.SMEM), vm, vm, any_, any_],
        out_specs=(vm, vm),
        scratch_shapes=[
            pltpu.VMEM((tiles, cells, cells), BF16),
            pltpu.VMEM((4, tiles, cells, cells), BF16),
            pltpu.VMEM((ROUNDS, CHUNKS, tiles, cells, cw), BF16),
            pltpu.VMEM((CHUNKS, tiles, cells, cw), F32),
            pltpu.VMEM((CHUNKS, tiles, cells, cw), F32),
            pltpu.VMEM((tiles * cells, width), BF16),
            pltpu.VMEM((tiles * cells, width), BF16),
            pltpu.VMEM((packed, cw), F32),
            pltpu.VMEM((packed, cw), F32),
            *[pltpu.VMEM((size // 2 if halve else size, cw), F32) for _, _, size, halve in stages],
            dma((2,)),
            dma((ndir, ROUNDS, CHUNKS)),
            dma((ndir, ROUNDS, CHUNKS)),
            dma((len(stages),)),
            dma((len(stages),)),
            dma((len(stages),)),
            dma((len(stages),)),
            *[pltpu.VMEM((tiles, cells, cw), BF16)] * (ndir * ROUNDS * CHUNKS),
        ],
        compiler_params=pltpu.CompilerParams(collective_id=0, has_side_effects=True),
        name="filter",
    )(couple_map[0, 0], cell_scale[0, 0][..., None], initial_block[0, 0], tile_ops[0, 0], couple_ops[0, 0])
    basis, factor = orthonormalize(gram, y.reshape(tiles * cells, width), tiles * cells * ny * nz)
    return basis.reshape(shape), factor


def solution(mesh):
    placed = (
        P("gy", "gz", None, None, None),
        P("gy", "gz", None, None, None),
        P("gy", "gz", None, None, None, None),
        P("gy", "gz", None, None),
        P("gy", "gz", None, None),
    )
    return jax.shard_map(
        functools.partial(body, mesh.shape["gy"], mesh.shape["gz"]),
        mesh=mesh,
        in_specs=placed,
        out_specs=(P("gy", "gz", None, None, None), P()),
        check_vma=False,
    )
```

time: 439 us -> 164 us (0.37); the launches traced: 433 us -> 163 us
  waiting for transfers between devices: 189 us -> 0 us
  Pallas kernels: 0 us -> 160 us
  other arithmetic: 132 us -> 0 us
  matrix products: 45.4 us -> 0 us
  local copies, waits for them, and re-layouts: 29.7 us -> 3.04 us
  starting transfers between devices: 19.4 us -> 0 us
  between operations: 17.2 us -> 0.64 us
    pallas_call x0 -> x2, Pallas kernels: none -> 160 us  [the longest x1 115 us: body(): pl.pallas_call(functools.partial(filter_kernel, ny, nz, stages, width), o...]
    psum x1 -> x0, waiting for transfers between devices: 131 us -> none  [body(): gram = lax.psum(local_gram, ('gy', 'gz'))]
    another operation x19 -> x0, other arithmetic: 127 us -> none  [the longest x14 78.7 us: body(): lower = jnp.linalg.cholesky(gram)]
    ppermute x9 -> x0, waiting for transfers between devices: 58.7 us -> none  [shifted(): return lax.ppermute(block, axis, route)]
    dot_general x7 -> x0, matrix products: 31.2 us -> none  [the longest x3 23.3 us: apply_scaled(): jnp.einsum('dtij,dtjk->tik', couple_ops[0, 0], picked, preferred_element_...]
    ppermute x9 -> x0, starting transfers between devices: 19.3 us -> none  [shifted(): return lax.ppermute(block, axis, route)]
    gather x5 -> x0, local copies, waits for them, and re-layouts: 15.2 us -> none  [pick_tiles(): return jnp.take(blocks, indices, axis=0)]
    another operation x13 -> x0, matrix products: 14.1 us -> none  [the longest x7 12.2 us: body(): basis = jax.scipy.linalg.solve_triangular(lower, flat.T, lower=True).T]
  transfers between devices with their start and end apart: 10 -> 0, of which waited for: 7 -> 0; matrix products, arithmetic and copies ran while one was open for 1% -> 0% of each run, Pallas kernels for 0% -> 0%
where the time goes in v1:
time: 164 us; the launch traced here: 163 us
  Pallas kernels  160 us (98%)
  local copies, waits for them, and re-layouts  3.04 us (2%)
    pallas_call x1, Pallas kernels, body(): pl.pallas_call(functools.partial(filter_kernel, ny, nz, stages, width), o...  115 us
    pallas_call x1, Pallas kernels, orthonormalize(): pl.pallas_call(functools.partial(ortho_kernel, total_cells), out_shape=(j...  45.1 us

profile of v1, /device:TPU:0, one launch (start us, length us, event | category | flops | bytes accessed | tf_op | source)
XLA Modules:
  0.0 163.5 jit_solution(61682775283729826)
XLA Ops:
  0.6 1.3 copy.8.map_ref
  2.0 1.7 %copy.9.scale_ref = f32[2,512,1]{2,1,0:T(8,128)} copy(f32[2,512,1]{1,0,2:T(2,128)} %bitcast.11) | data formatting | bytes 8192 | tf_op jit(solution)/shard_map/broadcast_in_dim;squeeze | solution.py:349
  3.7 114.7 %filter.1 = (f32[2,512,512]{2,1,0:T(8,128)}, f32[768,256]{1,0:T(8,128)}) custom-call(s32[4,2]{1,0:T(4,128)} %copy.8.map_ref, f32[2,512,1]{2,1,0:T(8,128)} %copy.9.scale_ref, bf16[2,512,512]{2,1,0:T(8,128)(2,1)} %bitcast.9, bf16[2,512,512]{2,1,0:T(8,128)(2,1)} %bitcast.10, bf16[4,2,512,512]{3,2,1,0:T(8,128)(2,1)} %bitcast.7), custom_call_target="tpu_custom_call" | custom-call | tf_op jit(solution)/shard_map/filter/pallas_call | solution.py:319
  118.4 45.1 %ortho.1 = (f32[1024,512]{1,0:T(8,128)}, f32[512,512]{1,0:T(8,128)}) custom-call(f32[768,256]{1,0:T(8,128)} %get-tuple-element.6.gram_ref, f32[1024,512]{1,0:T(8,128)} %bitcast.8), custom_call_target="tpu_custom_call" | custom-call | tf_op jit(solution)/shard_map/ortho/pallas_call | solution.py:294

commit v2 on v1

--- a/solution.py
+++ b/solution.py
@@ -12,7 +12,7 @@
 ROUNDS = 3
 CHUNKS = 2
 BASE = 128
-PANEL = 8
+PANEL = 32
 
 
 def split(x):
@@ -20,25 +20,44 @@
     return hi, (x - hi.astype(F32)).astype(BF16)
 
 
+def packed(i, j):
+    place = j * (j + 1) // 2 + i
+    return slice(place * BASE, (place + 1) * BASE)
+
+
 def xor_stages(ny, nz, rows):
-    order = [("gy", 0)]
-    order += [("gz", b) for b in range(nz.bit_length() - 1)]
-    order += [("gy", b) for b in range(1, ny.bit_length() - 1)]
+    ybits = [("gy", b) for b in range(ny.bit_length() - 1)]
+    zbits = [("gz", b) for b in range(nz.bit_length() - 1)]
+    groups = [ybits[:1], zbits[:1] + ybits[1:2]]
+    left = ybits[2:] + zbits[1:]
+    groups += [left[n:n + 2] for n in range(0, len(left), 2)]
     stages, size = [], rows
-    for axis, bit in order:
-        halve = size % 16 == 0
-        stages.append((axis, bit, size, halve))
-        size = size // 2 if halve else size
+    for group in groups:
+        if size % (8 << len(group)) == 0:
+            stages.append((tuple(group), size, True))
+            size >>= len(group)
+            continue
+        for bit in group:
+            halve = size % 16 == 0
+            stages.append(((bit,), size, halve))
+            size = size // 2 if halve else size
     return stages
+
+
+def part_of(stage):
+    bits, size, halve = stage
+    return size >> len(bits) if halve else size
 
 
 def filter_kernel(
     ny, nz, stages, nvec,
-    map_ref, scale_ref, first_ref, tile_hbm, couple_hbm,
-    y_ref, gram_ref,
-    tile_ref, couple_ref, sent, second, third, hi, lo, gsum, gall, *rest,
+    map_ref, scale_row, first_ref, tile_hbm, couple_hbm,
+    y_hbm, gram_ref,
+    y_ref, scale_wide, tile_ref, couple_ref, sent, second, third, hi, lo, gsum, gall, *rest,
 ):
-    pieces, rest = rest[: len(stages)], rest[len(stages):]
+    peers = [(n, m) for n, stage in enumerate(stages) for m in range(1, 1 << len(stage[0]))]
+    pieces, rest = dict(zip(peers, rest)), rest[len(peers):]
+    index = {peer: k for k, peer in enumerate(peers)}
     op_sem, send_sem, recv_sem, rs_send, rs_recv, ag_send, ag_recv, *landed = rest
     got = {
         (d, r, c): landed[(d * ROUNDS + r) * CHUNKS + c]
@@ -49,10 +68,18 @@
     iy, iz = lax.axis_index("gy"), lax.axis_index("gz")
     where = {"gy": iy, "gz": iz}
 
-    def partner(axis, bit):
-        me = where[axis]
-        b = (me // (2**bit)) % 2
-        return {axis: me + (1 - 2 * b) * (2**bit)}, b
+    def code_of(bits):
+        return sum(((where[axis] // (2**bit)) % 2) * 2**k for k, (axis, bit) in enumerate(bits))
+
+    def partner(bits, m):
+        device, code = {}, 0
+        for k, (axis, bit) in enumerate(bits):
+            b = (where[axis] // (2**bit)) % 2
+            if (m >> k) & 1:
+                device[axis] = device.get(axis, where[axis]) + (1 - 2 * b) * (2**bit)
+                b = 1 - b
+            code = code + b * 2**k
+        return device, code
 
     targets = [{"gy": (iy + 1) % ny}, {"gy": (iy + ny - 1) % ny}]
     if nz == 2:
@@ -70,7 +97,7 @@
         copy.start()
 
     barrier = pltpu.get_barrier_semaphore()
-    greeted = targets + [partner(axis, bit)[0] for axis, bit, _, _ in stages]
+    greeted = targets + [partner(stages[n][0], m)[0] for n, m in peers]
     for other in greeted:
         pl.semaphore_signal(barrier, inc=1, device_id=other, device_id_type=MESH)
 
@@ -89,24 +116,36 @@
             made.append(copy)
         return made
 
+    for t in range(tiles):
+        scale_wide[t] = jnp.broadcast_to(scale_row[t:t + 1, :], (BASE, cells)).T
+
+    def scale_ref(t):
+        return jnp.concatenate([scale_wide[t]] * (cw // BASE), axis=1)
+
     moving = {}
     for c in range(CHUNKS):
         for t in range(tiles):
-            sent[0, c, t] = (scale_ref[t] * first_ref[t, :, c * cw:(c + 1) * cw].astype(F32)).astype(BF16)
+            sent[0, c, t] = (scale_ref(t) * first_ref[t, :, c * cw:(c + 1) * cw].astype(F32)).astype(BF16)
         if c == 0:
             pl.semaphore_wait(barrier, len(greeted))
         moving[0, c] = send(0, c)
     for copy in copies_in:
         copy.wait()
 
-    def gram_of(i, j, place):
+    def gram_of(i, j):
         def dot(a, b):
             return lax.dot_general(a, b, (((0,), (0,)), ((), ())), preferred_element_type=F32)
         left, right = slice(i * cw, (i + 1) * cw), slice(j * cw, (j + 1) * cw)
         total = dot(hi[:, left], hi[:, right])
         total += dot(hi[:, left], lo[:, right])
         total += dot(lo[:, left], hi[:, right])
-        gsum[place * cw:(place + 1) * cw] = total
+        per = cw // BASE
+        for a in range(per):
+            for b in range(per):
+                if i * per + a <= j * per + b:
+                    gsum[packed(i * per + a, j * per + b)] = total[
+                        a * BASE:(a + 1) * BASE, b * BASE:(b + 1) * BASE
+                    ]
 
     for r in range(ROUNDS):
         for c in range(CHUNKS):
@@ -120,7 +159,7 @@
                     acc += jnp.dot(
                         couple_ref[d, t], got[slot[d], r, c][map_ref[d, t]], preferred_element_type=F32
                     )
-                s = scale_ref[t]
+                s = scale_ref(t)
                 if r == 0:
                     y = first_ref[t, :, cols].astype(F32)
                 elif r == 1:
@@ -149,53 +188,65 @@
             if r < ROUNDS - 1:
                 moving[r + 1, c] = send(r + 1, c)
             else:
-                place = c * (c + 1) // 2
                 for i in range(c + 1):
-                    gram_of(i, c, place + i)
+                    gram_of(i, c)
+    y_out = pltpu.make_async_copy(y_ref, y_hbm, op_sem.at[2])
+    y_out.start()
 
     base = 0
-    for n, (axis, bit, size, halve) in enumerate(stages):
-        other, b = partner(axis, bit)
-        part = size // 2 if halve else size
-        out = base + (1 - b) * part if halve else base
-        keep = base + b * part if halve else base
-        copy = pltpu.make_async_remote_copy(
-            src_ref=gsum.at[pl.ds(pl.multiple_of(out, 8), part)],
-            dst_ref=pieces[n],
-            send_sem=rs_send.at[n],
-            recv_sem=rs_recv.at[n],
-            device_id=other,
-            device_id_type=MESH,
-        )
-        copy.start()
-        copy.wait()
-        here = pl.ds(pl.multiple_of(keep, 8), part)
-        gsum[here] = gsum[here] + pieces[n][...]
-        base = keep
-    last = stages[-1][2] // 2 if stages[-1][3] else stages[-1][2]
-    here = pl.ds(pl.multiple_of(base, 8), last)
+    for n, (bits, size, halve) in enumerate(stages):
+        part = part_of(stages[n])
+        copies = []
+        for m in range(1, 1 << len(bits)):
+            other, code = partner(bits, m)
+            start = base + code * part if halve else base
+            copy = pltpu.make_async_remote_copy(
+                src_ref=gsum.at[pl.ds(pl.multiple_of(start, 8), part)],
+                dst_ref=pieces[n, m],
+                send_sem=rs_send.at[index[n, m]],
+                recv_sem=rs_recv.at[index[n, m]],
+                device_id=other,
+                device_id_type=MESH,
+            )
+            copy.start()
+            copies.append(copy)
+        for copy in copies:
+            copy.wait()
+        if halve:
+            base = base + code_of(bits) * part
+        here = pl.ds(pl.multiple_of(base, 8), part)
+        total = gsum[here]
+        for m in range(1, 1 << len(bits)):
+            total = total + pieces[n, m][...]
+        gsum[here] = total
+    here = pl.ds(pl.multiple_of(base, 8), part_of(stages[-1]))
     gall[here] = gsum[here]
     for n in reversed(range(len(stages))):
-        axis, bit, size, halve = stages[n]
+        bits, size, halve = stages[n]
         if not halve:
             continue
-        other, b = partner(axis, bit)
-        here = pl.ds(pl.multiple_of(base, 8), size // 2)
-        copy = pltpu.make_async_remote_copy(
-            src_ref=gall.at[here],
-            dst_ref=gall.at[here],
-            send_sem=ag_send.at[n],
-            recv_sem=ag_recv.at[n],
-            device_id=other,
-            device_id_type=MESH,
-        )
-        copy.start()
-        copy.wait()
-        base = base - b * (size // 2)
+        part = part_of(stages[n])
+        here = pl.ds(pl.multiple_of(base, 8), part)
+        copies = []
+        for m in range(1, 1 << len(bits)):
+            copy = pltpu.make_async_remote_copy(
+                src_ref=gall.at[here],
+                dst_ref=gall.at[here],
+                send_sem=ag_send.at[index[n, m]],
+                recv_sem=ag_recv.at[index[n, m]],
+                device_id=partner(bits, m)[0],
+                device_id_type=MESH,
+            )
+            copy.start()
+            copies.append(copy)
+        for copy in copies:
+            copy.wait()
+        base = base - code_of(bits) * part
     gram_ref[...] = gall[...]
     for made in moving.values():
         for copy in made:
             copy.wait_send()
+    y_out.wait()
 
 
 def factor_block(work):
@@ -232,10 +283,11 @@
     lax.fori_loop(0, BASE // PANEL, panel, 0)
 
 
-def ortho_kernel(total_cells, gram_ref, y_ref, basis_ref, factor_ref, full, work):
+def ortho_kernel(total_cells, gram_ref, y_hbm, basis_hbm, factor_ref, full, work, y_ref, basis_ref, y_sem, out_sem):
     width = factor_ref.shape[0]
-    cw = width // CHUNKS
     count = width // BASE
+    y_in = pltpu.make_async_copy(y_hbm, y_ref, y_sem)
+    y_in.start()
 
     def dot(a, b, dims):
         return lax.dot_general(
@@ -243,11 +295,10 @@
         )
 
     full[...] = jnp.zeros_like(full)
-    for c in range(CHUNKS):
-        for i in range(c + 1):
-            place = c * (c + 1) // 2 + i
-            full[i * cw:(i + 1) * cw, c * cw:(c + 1) * cw] = (
-                gram_ref[place * cw:(place + 1) * cw] / jnp.float32(total_cells)
+    for j in range(count):
+        for i in range(j + 1):
+            full[i * BASE:(i + 1) * BASE, j * BASE:(j + 1) * BASE] = (
+                gram_ref[packed(i, j)] / jnp.float32(total_cells)
             )
     eye = (
         lax.broadcasted_iota(jnp.int32, (BASE, BASE), 0)
@@ -276,17 +327,20 @@
     factor_ref[...] = jnp.where(tri, full[:, :width], 0.0)
     ih, il = split(full[:, width:])
 
-    def rows_of(n, carry):
-        here = pl.ds(pl.multiple_of(n * 256, 256), 256)
+    def half(a, b):
+        return lax.dot_general(a, b, (((1,), (1,)), ((), ())), preferred_element_type=F32)
+
+    y_in.wait()
+    outs = []
+    for n in range(y_ref.shape[0] // 256):
+        here = pl.ds(n * 256, 256)
         yh, yl = split(y_ref[here])
-
-        def half(a, b):
-            return lax.dot_general(a, b, (((1,), (1,)), ((), ())), preferred_element_type=F32)
-
         basis_ref[here] = half(yh, ih) + half(yh, il) + half(yl, ih)
-        return carry
-
-    lax.fori_loop(0, y_ref.shape[0] // 256, rows_of, 0)
+        copy = pltpu.make_async_copy(basis_ref.at[here], basis_hbm.at[here], out_sem.at[n])
+        copy.start()
+        outs.append(copy)
+    for copy in outs:
+        copy.wait()
 
 
 def orthonormalize(gram, y, total_cells):
@@ -297,11 +351,15 @@
             jax.ShapeDtypeStruct(y.shape, F32),
             jax.ShapeDtypeStruct((width, width), F32),
         ),
-        in_specs=[pl.BlockSpec(memory_space=pltpu.VMEM)] * 2,
-        out_specs=(pl.BlockSpec(memory_space=pltpu.VMEM),) * 2,
+        in_specs=[pl.BlockSpec(memory_space=pltpu.VMEM), pl.BlockSpec(memory_space=pl.ANY)],
+        out_specs=(pl.BlockSpec(memory_space=pl.ANY), pl.BlockSpec(memory_space=pltpu.VMEM)),
         scratch_shapes=[
             pltpu.VMEM((width, 2 * width), F32),
             pltpu.VMEM((BASE, 2 * BASE), F32),
+            pltpu.VMEM(y.shape, F32),
+            pltpu.VMEM(y.shape, F32),
+            pltpu.SemaphoreType.DMA,
+            pltpu.SemaphoreType.DMA((y.shape[0] // 256,)),
         ],
         name="ortho",
     )(gram, y)
@@ -311,8 +369,10 @@
     shape = initial_block.shape
     tiles, cells, width = shape[2:]
     cw = width // CHUNKS
-    packed = CHUNKS * (CHUNKS + 1) // 2 * cw
-    stages = xor_stages(ny, nz, packed)
+    count = width // BASE
+    rows = count * (count + 1) // 2 * BASE
+    stages = xor_stages(ny, nz, rows)
+    parts = [part_of(stage) for stage in stages for _ in range(1, 1 << len(stage[0]))]
     ndir = 3 if nz == 2 else 4
     vm, any_ = pl.BlockSpec(memory_space=pltpu.VMEM), pl.BlockSpec(memory_space=pl.ANY)
     dma = pltpu.SemaphoreType.DMA
@@ -320,11 +380,13 @@
         functools.partial(filter_kernel, ny, nz, stages, width),
         out_shape=(
             jax.ShapeDtypeStruct((tiles, cells, width), F32),
-            jax.ShapeDtypeStruct((packed, cw), F32),
+            jax.ShapeDtypeStruct((rows, BASE), F32),
         ),
         in_specs=[pl.BlockSpec(memory_space=pltpu.SMEM), vm, vm, any_, any_],
-        out_specs=(vm, vm),
+        out_specs=(any_, vm),
         scratch_shapes=[
+            pltpu.VMEM((tiles, cells, width), F32),
+            pltpu.VMEM((tiles, cells, BASE), F32),
             pltpu.VMEM((tiles, cells, cells), BF16),
             pltpu.VMEM((4, tiles, cells, cells), BF16),
             pltpu.VMEM((ROUNDS, CHUNKS, tiles, cells, cw), BF16),
@@ -332,21 +394,21 @@
             pltpu.VMEM((CHUNKS, tiles, cells, cw), F32),
             pltpu.VMEM((tiles * cells, width), BF16),
             pltpu.VMEM((tiles * cells, width), BF16),
-            pltpu.VMEM((packed, cw), F32),
-            pltpu.VMEM((packed, cw), F32),
-            *[pltpu.VMEM((size // 2 if halve else size, cw), F32) for _, _, size, halve in stages],
-            dma((2,)),
+            pltpu.VMEM((rows, BASE), F32),
+            pltpu.VMEM((rows, BASE), F32),
+            *[pltpu.VMEM((part, BASE), F32) for part in parts],
+            dma((3,)),
             dma((ndir, ROUNDS, CHUNKS)),
             dma((ndir, ROUNDS, CHUNKS)),
-            dma((len(stages),)),
-            dma((len(stages),)),
-            dma((len(stages),)),
-            dma((len(stages),)),
+            dma((len(parts),)),
+            dma((len(parts),)),
+            dma((len(parts),)),
+            dma((len(parts),)),
             *[pltpu.VMEM((tiles, cells, cw), BF16)] * (ndir * ROUNDS * CHUNKS),
         ],
         compiler_params=pltpu.CompilerParams(collective_id=0, has_side_effects=True),
         name="filter",
-    )(couple_map[0, 0], cell_scale[0, 0][..., None], initial_block[0, 0], tile_ops[0, 0], couple_ops[0, 0])
+    )(couple_map[0, 0], cell_scale[0, 0], initial_block[0, 0], tile_ops[0, 0], couple_ops[0, 0])
     basis, factor = orthonormalize(gram, y.reshape(tiles * cells, width), tiles * cells * ny * nz)
     return basis.reshape(shape), factor
 

time: 164 us -> 132 us (0.80)
  Pallas kernels: 160 us -> 130 us
  local copies, waits for them, and re-layouts: 3.04 us -> 1.34 us
    pallas_call x1, Pallas kernels: 45.1 us -> 27.6 us  [orthonormalize(): pl.pallas_call(functools.partial(ortho_kernel, total_cells), out_shape=(j...]
    pallas_call x1, Pallas kernels: 115 us -> 102 us  [body(): pl.pallas_call(functools.partial(filter_kernel, ny, nz, stages, width), o...]
    another operation x1 -> x0, local copies, waits for them, and re-layouts: 1.71 us -> none  [body(): cell_scale[0, 0][..., None]]
where the time goes in v2:
time: 132 us
  Pallas kernels  130 us (98%)
  local copies, waits for them, and re-layouts  1.34 us (1%)
    pallas_call x1, Pallas kernels, body(): pl.pallas_call(functools.partial(filter_kernel, ny, nz, stages, width), o...  102 us
    pallas_call x1, Pallas kernels, orthonormalize(): pl.pallas_call(functools.partial(ortho_kernel, total_cells), out_shape=(j...  27.6 us

profile of v2, /device:TPU:0, one launch (start us, length us, event | category | flops | bytes accessed | tf_op | source)
XLA Modules:
  0.0 131.8 jit_solution(9922211392601865464)
XLA Ops:
  0.6 1.3 %copy.7.map_ref = s32[4,2]{1,0:T(4,128)} copy(s32[4,2]{0,1:T(2,128)} %bitcast.12) | data formatting | bytes 64 | tf_op jit(solution)/shard_map/squeeze | solution.py:411
  2.0 102.2 %filter.1 = (f32[2,512,512]{2,1,0:T(8,128)}, f32[1280,128]{1,0:T(8,128)}) custom-call(s32[4,2]{1,0:T(4,128)} %copy.7.map_ref, f32[2,512]{1,0:T(2,128)} %bitcast.11, bf16[2,512,512]{2,1,0:T(8,128)(2,1)} %bitcast.9, bf16[2,512,512]{2,1,0:T(8,128)(2,1)} %bitcast.10, bf16[4,2,512,512]{3,2,1,0:T(8,128)(2,1)} %bitcast.7), custom_call_target="tpu_custom_call" | custom-call | tf_op jit(solution)/shard_map/filter/pallas_call | solution.py:379
  104.2 27.6 %ortho.1 = (f32[1024,512]{1,0:T(8,128)}, f32[512,512]{1,0:T(8,128)}) custom-call(f32[1280,128]{1,0:T(8,128)} %get-tuple-element.6.gram_ref, f32[1024,512]{1,0:T(8,128)} %bitcast.8), custom_call_target="tpu_custom_call" | custom-call | tf_op jit(solution)/shard_map/ortho/pallas_call | solution.py:348
